TPU v7x, 512 devices: a whole 4x8x8 slice. The times are simulated.
512 devices in a mesh: dp: 32 (over x, y_lo, core), mp: 16 (over z, y_hi).
Axes of the slice: x: 4, y: 8 (y_hi: 2, y_lo: 4; y = y_hi * 4 + y_lo), z: 8, core: 2. Of those that a mesh axis runs over, the one named last changes fastest.
Arguments:
- features: bfloat16 [57344, 1024], P(('dp', 'mp')), may hold values from -6 to 6
- row_position: int32 [57344], P(('dp', 'mp')), may hold values from 0 to 2047, as said below
- proj_weight: bfloat16 [1024, 8192], P(None, 'mp'), may hold values from -0.1875 to 0.1875
- proj_bias: float32 [8192], P('mp'), may hold values from -3 to 3
- norm_gain: float32 [8192], replicated, may hold values from 0.5 to 1.5
- cotangent: bfloat16 [65536, 8192], P(('dp', 'mp')), may hold values from -0.03125 to 0.03125
Outputs:
- grad_weight: bfloat16 [1024, 8192], P(None, 'mp')
- grad_bias: float32 [8192], P('mp')
Inputs may be any that keep to these rules, and one draw needn't show every extreme that they name: `row_position`: within each sequence's block of 1792 entries the positions are distinct; every such block holds position 0 and position 2047.
All inputs are finite; a program needn't handle non-finite values.
Results may differ from a plain program's by a relative error of at most 0.0059.
Values may be sent and summed in bfloat16 or wider, within the bound.
No kernel may reach another device: no remote copies, remote signals or barrier semaphores. Data moves between devices by JAX's collectives and lax.ppermute only.
A program may use at most 64 MiB of HBM per device.

v0:
```python
import jax
import jax.numpy as jnp
from jax import lax
from jax.sharding import PartitionSpec as P

EPSILON = 1e-05


def gelu_pair(pre_act):
    normal_cdf = 0.5 * (1.0 + lax.erf(pre_act * 0.7071067811865476))
    normal_pdf = jnp.exp(-0.5 * pre_act * pre_act) * 0.3989422804014327
    return (pre_act * normal_cdf, normal_cdf + pre_act * normal_pdf)


def per_device(features, row_position, proj_weight, proj_bias, norm_gain, cotangent):
    width = proj_weight.shape[1]
    seq_len = cotangent.shape[0] * lax.axis_size("mp")
    places = lax.all_gather(row_position, "mp", axis=0, tiled=True)
    total = places.shape[0]
    all_feats = lax.all_gather(features, "mp", axis=0, tiled=True)
    pre_act = jnp.dot(all_feats, proj_weight, preferred_element_type=jnp.float32) + proj_bias
    activated, slope = gelu_pair(pre_act)
    projected = activated.astype(jnp.bfloat16)
    source = (
        jnp.full((seq_len,), total, jnp.int32).at[places].set(jnp.arange(total, dtype=jnp.int32))
    )
    padded = jnp.concatenate([projected, jnp.zeros((1, width), jnp.bfloat16)], axis=0)
    outgoing = padded[source]
    embed = lax.all_to_all(outgoing, "mp", split_axis=0, concat_axis=1, tiled=True)
    embed_wide = lax.optimization_barrier(embed).astype(jnp.float32)
    inv_rms = lax.rsqrt(jnp.mean(embed_wide * embed_wide, axis=1, keepdims=True) + EPSILON)
    scaled_cot = cotangent.astype(jnp.float32) * norm_gain
    gdot = jnp.mean(scaled_cot * embed_wide, axis=1, keepdims=True)
    grad_embed = (inv_rms * scaled_cot - embed_wide * inv_rms * inv_rms * inv_rms * gdot).astype(
        jnp.bfloat16
    )
    returned = lax.all_to_all(grad_embed, "mp", split_axis=1, concat_axis=0, tiled=True)
    grad_proj = lax.optimization_barrier(returned[places]).astype(jnp.float32)
    grad_pre = (grad_proj * slope).astype(jnp.bfloat16)
    bias_grad = jnp.sum(grad_pre.astype(jnp.float32), axis=0)
    weight_grad = lax.dot_general(
        all_feats, grad_pre, (((0,), (0,)), ((), ())), preferred_element_type=jnp.float32
    )
    weight_grad, bias_grad = lax.psum((weight_grad, bias_grad), "dp")
    return (weight_grad.astype(jnp.bfloat16), bias_grad)


def solution(mesh):
    return jax.shard_map(
        per_device,
        mesh=mesh,
        in_specs=(
            P(("dp", "mp"), None),
            P(("dp", "mp")),
            P(None, "mp"),
            P("mp"),
            P(),
            P(("dp", "mp"), None),
        ),
        out_specs=(P(None, "mp"), P("mp")),
        check_vma=False,
    )
```

profile of v0, /device:TPU:64, one launch (start us, length us, event | category | flops | bytes accessed | tf_op | source)
XLA Modules:
  0.0 493.4 jit_solution(16986138296196837244)
XLA Ops:
  7.2 0.0 copy-start
  7.2 0.0 all-gather.2.cloned.1.call-start
  7.2 0.7 all-gather.2.cloned.1.call-update
  7.9 1.3 dynamic-slice
  9.8 0.9 dynamic-update-slice
  10.7 24.4 %all-reduce.1 = s32[1792]{0:T(1024)S(1)} all-reduce(s32[1792]{0:T(1024)S(1)} %dynamic-update-slice), channel_id=1, replica_groups=mesh['dp'=32,'mp'=16] {'mp'}, use_global_device_ids=true, to_apply=%add.1 | all-reduce | flops 1792 | bytes 14336
  35.1 7.1 %scatter_custom_fusion = s32[2048]{0:T(1024)S(1)} fusion(s32[1792]{0:T(1024)S(1)} %compare_select_fusion.1, s32[1792]{0:T(1024)S(1)} %iota.3, s32[]{:T(128)} %constant.5.clone.1), kind=kCustom, calls=%fused_computation.30 | custom fusion | bytes 8196 | tf_op jit(solution)/shard_map/scatter | solution.py:25
  42.3 98.6 %all-gather.2.cloned.1.call-done = bf16[1792,1024]{1,0:T(8,128)(2,1)} async-done(((bf16[112,1024]{1,0:T(8,128)(2,1)}), bf16[1792,1024]{1,0:T(8,128)(2,1)}) %all-gather.2.cloned.1.call-update) | async-done | bytes 3670032 | tf_op jit(solution)/shard_map/all_gather | solution.py:20
  140.9 0.0 copy-done
  140.9 5.9 %multiply_convert_fusion = (bf16[1792,512]{1,0:T(8,128)(2,1)S(1)}, f32[1792,512]{1,0:T(8,128)}) fusion(f32[512]{0:T(512)} %param.9, bf16[1792,1024]{1,0:T(8,128)(2,1)} %all-gather.2.cloned.1.call-done, bf16[1024,512]{1,0:T(8,128)(2,1)S(1)} %copy-done), kind=kOutput, calls=%fused_computation.22 | convolution fusion | flops 1884553216 | bytes 10225664 | tf_op jit(solution)/shard_map/dot_general | solution.py:21
  146.7 0.1 concatenate.3
  146.8 9.2 %gather_fusion = bf16[2048,512]{1,0:T(8,128)(2,1)} fusion(bf16[1793,512]{1,0:T(8,128)(2,1)S(1)} %concatenate.3, s32[2048]{0:T(1024)S(1)} %fusion.13), kind=kCustom, calls=%fused_computation | custom fusion | bytes 4202496 | tf_op jit(solution)/shard_map/gather | solution.py:28
  156.0 0.0 copy-start.1
  156.0 0.0 copy-start.2
  156.0 47.0 %all_to_all.38 = bf16[16,128,512]{2,1,0:T(8,128)(2,1)S(1)} all-to-all(bf16[16,128,512]{2,1,0:T(8,128)(2,1)} %bitcast.22), channel_id=1, replica_groups=mesh['dp'=32,'mp'=16] {'mp'}, dimensions={0} | all-to-all | bytes 4194304 | tf_op jit(solution)/shard_map/all_to_all | solution.py:29
  203.0 0.2 copy.12
  203.2 0.0 copy-done.1
  203.3 0.0 copy-done.2
  203.3 1.1 fusion
  204.4 1.4 fusion.5
  205.8 1.6 copy.14
  207.5 10.0 %all-to-all-start.1 = ((bf16[128,16,512]{2,0,1:T(8,128)(2,1)}), bf16[128,16,512]{2,0,1:T(8,128)(2,1)S(1)}, u32[]{:S(2)}, u32[]{:S(2)}) async-start(bf16[128,16,512]{2,0,1:T(8,128)(2,1)} %bitcast.23), calls=%async_computation.1 | async-start | bytes 4194304 | tf_op jit(solution)/shard_map/all_to_all | solution.py:37
  217.5 54.2 %all-to-all-done.1 = bf16[128,16,512]{2,0,1:T(8,128)(2,1)S(1)} async-done(((bf16[128,16,512]{2,0,1:T(8,128)(2,1)}), bf16[128,16,512]{2,0,1:T(8,128)(2,1)S(1)}, u32[]{:S(2)}, u32[]{:S(2)}) %all-to-all-start.1) | async-done | bytes 2097184 | tf_op jit(solution)/shard_map/all_to_all | solution.py:37
  271.8 0.0 copy-start.3
  271.8 6.1 %gather_fusion.1 = bf16[1792,512]{1,0:T(8,128)(2,1)} fusion(bf16[2048,512]{1,0:T(8,128)(2,1)S(1)} %bitcast.19, s32[2048]{0:T(1024)S(1)} %pad_clamp_fusion), kind=kCustom, calls=%fused_computation.1 | custom fusion | bytes 3677184 | tf_op jit(solution)/shard_map/gather | solution.py:38
  277.9 0.0 copy-done.3
  277.9 0.0 copy-start.4
  277.9 3.8 convert_reduce_fusion
  281.7 0.0 copy-done.4
  281.7 2.1 convolution_bitcast_fusion
  283.8 200.5 %all-reduce.4 = (bf16[1024,512]{0,1:T(8,128)(2,1)}, f32[512]{0:T(512)}) all-reduce(f32[1024,512]{0,1:T(8,128)S(1)} %convolution_bitcast_fusion, f32[512]{0:T(512)S(1)} %get-tuple-element.8), channel_id=1, replica_groups=mesh['dp'=32,'mp'=16] {'dp'}, use_global_device_ids=true, to_apply=%region_3.0 | all-reduce | flops 524800 | bytes 3149824 | tf_op jit(solution)/shard_map/psum | solution.py:44
  484.3 2.3 copy.10
  (6 shorter events, 0.0 us)
Async XLA Ops:
  7.2 133.7 %copy-start = (bf16[1024,512]{1,0:T(8,128)(2,1)S(1)}, bf16[1024,512]{1,0:T(8,128)(2,1)}, u32[]{:S(2)}) copy-start(bf16[1024,512]{1,0:T(8,128)(2,1)} %param.8) | copy-start | bytes 3145732
  7.2 133.7 %all-gather.2.cloned.1.call-start = ((), (), s32[]{:S(2)}) async-start(), calls=%async_computation.2 | async-start | bytes 3899392 | tf_op jit(solution)/shard_map/all_gather | solution.py:20
  156.0 47.3 %copy-start.1 = (bf16[128,8192]{1,0:T(8,128)(2,1)S(1)}, bf16[128,8192]{1,0:T(8,128)(2,1)}, u32[]{:S(2)}) copy-start(bf16[128,8192]{1,0:T(8,128)(2,1)} %param.11) | copy-start | bytes 6291460
  156.0 47.3 %copy-start.2 = (f32[8192]{0:T(1024)S(1)}, f32[8192]{0:T(1024)}, u32[]{:S(2)}) copy-start(f32[8192]{0:T(1024)} %param.10) | copy-start | bytes 98308
  207.5 64.3 %all-to-all-start.1 = ((bf16[128,16,512]{2,0,1:T(8,128)(2,1)}), bf16[128,16,512]{2,0,1:T(8,128)(2,1)S(1)}, u32[]{:S(2)}, u32[]{:S(2)}) async-start(bf16[128,16,512]{2,0,1:T(8,128)(2,1)} %bitcast.23), calls=%async_computation.1 | async-start | bytes 4194304 | tf_op jit(solution)/shard_map/all_to_all | solution.py:37
  271.8 6.1 %copy-start.3 = (f32[512]{0:T(512)S(1)}, f32[512]{0:T(512)}, u32[]{:S(2)}) copy-start(f32[512]{0:T(512)} %param.9) | copy-start | bytes 6148
  277.9 3.8 copy-start.4
Sparse Core Ops, SparseCore 0:
  11.2 129.6 all-gather.1
where the time goes:
time: 494 us; the launch traced here: 493 us
  blocking collectives  272 us (55%)
  waiting for transfers between devices  154 us (31%)
  local copies, waits for them, and re-layouts  28.8 us (6%)
  between operations  14.8 us (3%)
  starting transfers between devices  10.1 us (2%)
  matrix products  7.94 us (2%)
  other arithmetic  6.38 us (1%)
    psum x1, blocking collectives, per_device(): weight_grad, bias_grad = lax.psum((weight_grad, bias_grad), 'dp')  201 us
    all_gather x1, waiting for transfers between devices, per_device(): all_feats = lax.all_gather(features, 'mp', axis=0, tiled=True)  98.6 us
    all_to_all x1, waiting for transfers between devices, per_device(): lax.all_to_all(grad_embed, 'mp', split_axis=1, concat_axis=0, tiled=True)  54.2 us
    all_to_all x1, blocking collectives, per_device(): lax.all_to_all(outgoing, 'mp', split_axis=0, concat_axis=1, tiled=True)  47 us
    unnamed x1, blocking collectives  24.4 us
    all_to_all x1, starting transfers between devices, per_device(): lax.all_to_all(grad_embed, 'mp', split_axis=1, concat_axis=0, tiled=True)  10 us
  transfers between devices with their start and end apart: 2, of which 2 were waited for; matrix products, arithmetic and copies ran while one was open for 2% of the time, Pallas kernels for 0%

commit v1 on v0

--- a/solution.py
+++ b/solution.py
@@ -1,9 +1,22 @@
+import functools
 import jax
 import jax.numpy as jnp
 from jax import lax
 from jax.sharding import PartitionSpec as P
+from jax.lax import all_to_all, axis_size
 
 EPSILON = 1e-05
+
+
+def connect_forms(here_x, at_axis, axis_k):
+    main = jnp.concatenate(
+        all_to_all(jnp.stack(jnp.split(here_x, axis_size("mp"), axis=axis_k), 0), "mp", 0, 0),
+        axis=at_axis,
+    )
+    return main
+
+
+fill_the_chunk = functools.partial(connect_forms, at_axis=0, axis_k=1)
 
 
 def gelu_pair(pre_act):
@@ -34,7 +47,7 @@
     grad_embed = (inv_rms * scaled_cot - embed_wide * inv_rms * inv_rms * inv_rms * gdot).astype(
         jnp.bfloat16
     )
-    returned = lax.all_to_all(grad_embed, "mp", split_axis=1, concat_axis=0, tiled=True)
+    returned = fill_the_chunk(grad_embed)
     grad_proj = lax.optimization_barrier(returned[places]).astype(jnp.float32)
     grad_pre = (grad_proj * slope).astype(jnp.bfloat16)
     bias_grad = jnp.sum(grad_pre.astype(jnp.float32), axis=0)

time: 494 us -> 504 us (1.020)
  local copies, waits for them, and re-layouts: 28.8 us -> 39 us
    unnamed x14 -> x29, local copies, waits for them, and re-layouts: 4.44 us -> 15.6 us
where the time goes in v1:
time: 504 us
  blocking collectives  272 us (54%)
  waiting for transfers between devices  154 us (31%)
  local copies, waits for them, and re-layouts  39 us (8%)
  between operations  14.8 us (3%)
  starting transfers between devices  10.1 us (2%)
  matrix products  7.94 us (2%)
  other arithmetic  6.38 us (1%)
    psum x1, blocking collectives, per_device(): weight_grad, bias_grad = lax.psum((weight_grad, bias_grad), 'dp')  201 us
    all_gather x1, waiting for transfers between devices, per_device(): all_feats = lax.all_gather(features, 'mp', axis=0, tiled=True)  98.6 us
    all_to_all x1, waiting for transfers between devices, connect_forms(): all_to_all(jnp.stack(jnp.split(here_x, axis_size('mp'), axis=axis_k), 0),...  54.2 us
    all_to_all x1, blocking collectives, per_device(): lax.all_to_all(outgoing, 'mp', split_axis=0, concat_axis=1, tiled=True)  46.9 us
    unnamed x1, blocking collectives  24.4 us
    unnamed x29, local copies, waits for them, and re-layouts  15.6 us
  transfers between devices with their start and end apart: 2, of which 2 were waited for; matrix products, arithmetic and copies ran while one was open for 2% of the time, Pallas kernels for 0%

profile of v1, /device:TPU:64, one launch (start us, length us, event | category | flops | bytes accessed | tf_op | source)
XLA Modules:
  0.0 503.5 jit_solution(17934256153847902769)
XLA Ops:
  7.2 0.7 all-gather.2.cloned.1.call-update
  7.9 1.3 dynamic-slice
  9.8 0.9 dynamic-update-slice
  10.7 24.4 %all-reduce.1 = s32[1792]{0:T(1024)S(1)} all-reduce(s32[1792]{0:T(1024)S(1)} %dynamic-update-slice), channel_id=1, replica_groups=mesh['dp'=32,'mp'=16] {'mp'}, use_global_device_ids=true, to_apply=%add.1 | all-reduce | flops 1792 | bytes 14336
  35.1 7.1 %scatter_custom_fusion = s32[2048]{0:T(1024)S(1)} fusion(s32[1792]{0:T(1024)S(1)} %compare_select_fusion.1, s32[1792]{0:T(1024)S(1)} %iota.3, s32[]{:T(128)} %constant.5.clone.1), kind=kCustom, calls=%fused_computation.61 | custom fusion | bytes 8196 | tf_op jit(solution)/shard_map/scatter | solution.py:38
  42.3 98.6 %all-gather.2.cloned.1.call-done = bf16[1792,1024]{1,0:T(8,128)(2,1)} async-done(((bf16[112,1024]{1,0:T(8,128)(2,1)}), bf16[1792,1024]{1,0:T(8,128)(2,1)}) %all-gather.2.cloned.1.call-update) | async-done | bytes 3670032 | tf_op jit(solution)/shard_map/all_gather | solution.py:33
  140.9 5.9 %multiply_convert_fusion = (bf16[1792,512]{1,0:T(8,128)(2,1)S(1)}, f32[1792,512]{1,0:T(8,128)}) fusion(f32[512]{0:T(512)} %param.9, bf16[1792,1024]{1,0:T(8,128)(2,1)} %all-gather.2.cloned.1.call-done, bf16[1024,512]{1,0:T(8,128)(2,1)S(1)} %copy-done), kind=kOutput, calls=%fused_computation.22 | convolution fusion | flops 1884553216 | bytes 10225664 | tf_op jit(solution)/shard_map/dot_general | solution.py:34
  146.8 9.2 %gather_fusion = bf16[2048,512]{1,0:T(8,128)(2,1)} fusion(bf16[1793,512]{1,0:T(8,128)(2,1)S(1)} %concatenate.3, s32[2048]{0:T(1024)S(1)} %fusion.29), kind=kCustom, calls=%fused_computation | custom fusion | bytes 4202496 | tf_op jit(solution)/shard_map/gather | solution.py:41
  156.0 46.9 %all_to_all.24 = bf16[16,128,512]{2,1,0:T(8,128)(2,1)S(1)} all-to-all(bf16[16,128,512]{2,1,0:T(8,128)(2,1)} %bitcast.80), channel_id=1, replica_groups=mesh['dp'=32,'mp'=16] {'mp'}, dimensions={0} | all-to-all | bytes 4194304 | tf_op jit(solution)/shard_map/all_to_all | solution.py:42
  203.1 1.4 copy-done.1
  204.5 1.1 fusion
  205.6 1.4 fusion.5
  207.1 0.7 fusion.28
  207.7 0.7 fusion.27
  208.4 0.7 fusion.26
  209.0 0.6 fusion.25
  210.3 0.7 fusion.23
  211.0 0.7 fusion.22
  211.6 0.7 fusion.21
  212.3 0.7 fusion.20
  213.6 0.7 fusion.18
  214.9 0.7 fusion.16
  215.6 0.7 fusion.15
  216.2 0.7 fusion.14
  216.9 0.7 fusion.13
  217.6 10.0 %all-to-all-start.1 = ((bf16[16,128,512]{2,1,0:T(8,128)(2,1)}), bf16[16,128,512]{2,1,0:T(8,128)(2,1)S(1)}, u32[]{:S(2)}, u32[]{:S(2)}) async-start(bf16[16,128,512]{2,1,0:T(8,128)(2,1)} %fusion.13), calls=%async_computation.1 | async-start | bytes 4194304 | tf_op jit(solution)/shard_map/all_to_all | solution.py:13
  227.6 54.2 %all-to-all-done.1 = bf16[16,128,512]{2,1,0:T(8,128)(2,1)S(1)} async-done(((bf16[16,128,512]{2,1,0:T(8,128)(2,1)}), bf16[16,128,512]{2,1,0:T(8,128)(2,1)S(1)}, u32[]{:S(2)}, u32[]{:S(2)}) %all-to-all-start.1) | async-done | bytes 2097184 | tf_op jit(solution)/shard_map/all_to_all | solution.py:13
  281.9 6.1 %gather_fusion.1 = bf16[1792,512]{1,0:T(8,128)(2,1)} fusion(bf16[2048,512]{1,0:T(8,128)(2,1)S(1)} %bitcast.77, s32[2048]{0:T(1024)S(1)} %pad_clamp_fusion), kind=kCustom, calls=%fused_computation.1 | custom fusion | bytes 3677184 | tf_op jit(solution)/shard_map/gather | solution.py:51
  288.0 3.8 convert_reduce_fusion
  291.8 2.1 convolution_bitcast_fusion
  293.9 200.5 %all-reduce.4 = (bf16[1024,512]{0,1:T(8,128)(2,1)}, f32[512]{0:T(512)}) all-reduce(f32[1024,512]{0,1:T(8,128)S(1)} %convolution_bitcast_fusion, f32[512]{0:T(512)S(1)} %get-tuple-element.8), channel_id=1, replica_groups=mesh['dp'=32,'mp'=16] {'dp'}, use_global_device_ids=true, to_apply=%region_3.0 | all-reduce | flops 524800 | bytes 3149824 | tf_op jit(solution)/shard_map/psum | solution.py:57
  494.4 2.3 copy.9
  (21 shorter events, 2.4 us)
Async XLA Ops:
  7.2 133.7 %copy-start = (bf16[1024,512]{1,0:T(8,128)(2,1)S(1)}, bf16[1024,512]{1,0:T(8,128)(2,1)}, u32[]{:S(2)}) copy-start(bf16[1024,512]{1,0:T(8,128)(2,1)} %param.8) | copy-start | bytes 3145732
  7.2 133.7 %all-gather.2.cloned.1.call-start = ((), (), s32[]{:S(2)}) async-start(), calls=%async_computation.2 | async-start | bytes 3899392 | tf_op jit(solution)/shard_map/all_gather | solution.py:33
  202.9 1.6 copy-start.1
  202.9 1.6 copy-start.2
  217.6 64.3 %all-to-all-start.1 = ((bf16[16,128,512]{2,1,0:T(8,128)(2,1)}), bf16[16,128,512]{2,1,0:T(8,128)(2,1)S(1)}, u32[]{:S(2)}, u32[]{:S(2)}) async-start(bf16[16,128,512]{2,1,0:T(8,128)(2,1)} %fusion.13), calls=%async_computation.1 | async-start | bytes 4194304 | tf_op jit(solution)/shard_map/all_to_all | solution.py:13
  281.9 6.1 %copy-start.3 = (f32[512]{0:T(512)S(1)}, f32[512]{0:T(512)}, u32[]{:S(2)}) copy-start(f32[512]{0:T(512)} %param.9) | copy-start | bytes 6148
  288.0 3.8 copy-start.4
Sparse Core Ops, SparseCore 0:
  11.2 129.6 all-gather.1

commit v2 on v0

--- a/solution.py
+++ b/solution.py
@@ -4,6 +4,16 @@
 from jax.sharding import PartitionSpec as P
 
 EPSILON = 1e-05
+
+
+def shape_modes_on(piece_in, out_dim):
+    carry_out = lax.all_to_all(
+        jnp.stack(tuple((piece_in for _ in range(lax.axis_size("mp"))))),
+        axis_name="mp",
+        split_axis=0,
+        concat_axis=0,
+    )
+    return jnp.concatenate(carry_out, out_dim)
 
 
 def gelu_pair(pre_act):
@@ -17,7 +27,7 @@
     seq_len = cotangent.shape[0] * lax.axis_size("mp")
     places = lax.all_gather(row_position, "mp", axis=0, tiled=True)
     total = places.shape[0]
-    all_feats = lax.all_gather(features, "mp", axis=0, tiled=True)
+    all_feats = shape_modes_on(features, 0)
     pre_act = jnp.dot(all_feats, proj_weight, preferred_element_type=jnp.float32) + proj_bias
     activated, slope = gelu_pair(pre_act)
     projected = activated.astype(jnp.bfloat16)

time: 494 us -> 531 us (1.075)
  the two profiles are of different devices: /device:TPU:64 before, /device:TPU:32 now
where the time goes in v2:
time: 531 us; the launch traced here: 530 us
  blocking collectives  399 us (75%)
  waiting for transfers between devices  57 us (11%)
  local copies, waits for them, and re-layouts  31.5 us (6%)
  starting transfers between devices  24.9 us (5%)
  matrix products  10 us (2%)
  other arithmetic  6.23 us (1%)
    psum x1, blocking collectives, per_device(): weight_grad, bias_grad = lax.psum((weight_grad, bias_grad), 'dp')  239 us
    unnamed x1, blocking collectives  96.7 us
    all_to_all x1, blocking collectives, per_device(): lax.all_to_all(outgoing, 'mp', split_axis=0, concat_axis=1, tiled=True)  63.2 us
    all_to_all x1, waiting for transfers between devices, per_device(): lax.all_to_all(grad_embed, 'mp', split_axis=1, concat_axis=0, tiled=True)  57 us
    all_to_all x1, starting transfers between devices, shape_modes_on(): lax.all_to_all(jnp.stack(tuple((piece_in for _ in range(lax.axis_size('mp...  15.8 us
  transfers between devices with their start and end apart: 2, of which 1 were waited for; matrix products, arithmetic and copies ran while one was open for 2% of the time, Pallas kernels for 0%

profile of v2, /device:TPU:32, one launch (start us, length us, event | category | flops | bytes accessed | tf_op | source)
XLA Modules:
  0.0 530.2 jit_solution(6733188319794304451)
XLA Ops:
  0.6 0.0 copy-start
  0.6 3.3 stack.2
  4.0 0.0 copy-start.4
  4.0 0.0 copy-start.3
  4.0 15.8 %all-to-all-start = ((bf16[16,112,1024]{2,1,0:T(8,128)(2,1)}), bf16[16,112,1024]{2,1,0:T(8,128)(2,1)}, u32[]{:S(2)}, u32[]{:S(2)}) async-start(bf16[16,112,1024]{2,1,0:T(8,128)(2,1)} %stack.2), calls=%async_computation | async-start | bytes 7340032 | tf_op jit(solution)/shard_map/all_to_all | solution.py:10
  19.8 1.3 dynamic-slice
  21.7 0.0 copy-done.4
  21.7 0.3 dynamic-update-slice
  22.0 96.7 %all-reduce.1 = s32[1792]{0:T(1024)S(1)} all-reduce(s32[1792]{0:T(1024)S(1)} %dynamic-update-slice), channel_id=1, replica_groups=mesh['dp'=32,'mp'=16] {'mp'}, use_global_device_ids=true, to_apply=%add.1 | all-reduce | flops 1792 | bytes 14336
  118.7 7.1 %scatter_custom_fusion = s32[2048]{0:T(1024)S(1)} fusion(s32[1792]{0:T(1024)S(1)} %compare_select_fusion.1, s32[1792]{0:T(1024)S(1)} %iota.3, s32[]{:T(128)} %constant.5.clone.1), kind=kCustom, calls=%fused_computation.30 | custom fusion | bytes 8196 | tf_op jit(solution)/shard_map/scatter | solution.py:35
  125.9 0.0 all-to-all-done
  125.9 0.0 copy-done
  125.9 0.0 copy-done.3
  125.9 5.8 %multiply_convert_fusion = (bf16[1792,512]{1,0:T(8,128)(2,1)S(1)}, f32[1792,512]{1,0:T(8,128)}) fusion(f32[512]{0:T(512)S(1)} %copy-done.3, bf16[1792,1024]{1,0:T(8,128)(2,1)} %bitcast, bf16[1024,512]{1,0:T(8,128)(2,1)S(1)} %copy-done), kind=kOutput, calls=%fused_computation.22 | convolution fusion | flops 1884553216 | bytes 10225664 | tf_op jit(solution)/shard_map/dot_general | solution.py:31
  131.7 0.1 concatenate.3
  131.8 9.2 %gather_fusion = bf16[2048,512]{1,0:T(8,128)(2,1)} fusion(bf16[1793,512]{1,0:T(8,128)(2,1)S(1)} %concatenate.3, s32[2048]{0:T(1024)S(1)} %fusion.13), kind=kCustom, calls=%fused_computation | custom fusion | bytes 4202496 | tf_op jit(solution)/shard_map/gather | solution.py:38
  141.0 0.0 copy-start.1
  141.0 0.0 copy-start.2
  141.0 63.2 %all_to_all.43 = bf16[16,128,512]{2,1,0:T(8,128)(2,1)S(1)} all-to-all(bf16[16,128,512]{2,1,0:T(8,128)(2,1)} %bitcast.23), channel_id=1, replica_groups=mesh['dp'=32,'mp'=16] {'mp'}, dimensions={0} | all-to-all | bytes 4194304 | tf_op jit(solution)/shard_map/all_to_all | solution.py:39
  204.2 0.2 copy.12
  204.4 0.0 copy-done.1
  204.4 0.0 copy-done.2
  204.4 1.1 fusion
  205.6 1.4 fusion.5
  207.0 1.6 copy.14
  208.6 9.0 %all-to-all-start.2 = ((bf16[128,16,512]{2,0,1:T(8,128)(2,1)}), bf16[128,16,512]{2,0,1:T(8,128)(2,1)S(1)}, u32[]{:S(2)}, u32[]{:S(2)}) async-start(bf16[128,16,512]{2,0,1:T(8,128)(2,1)} %bitcast.24), calls=%async_computation.2 | async-start | bytes 4194304 | tf_op jit(solution)/shard_map/all_to_all | solution.py:47
  217.7 57.0 %all-to-all-done.2 = bf16[128,16,512]{2,0,1:T(8,128)(2,1)S(1)} async-done(((bf16[128,16,512]{2,0,1:T(8,128)(2,1)}), bf16[128,16,512]{2,0,1:T(8,128)(2,1)S(1)}, u32[]{:S(2)}, u32[]{:S(2)}) %all-to-all-start.2) | async-done | bytes 2097184 | tf_op jit(solution)/shard_map/all_to_all | solution.py:47
  274.6 6.1 %gather_fusion.1 = bf16[1792,512]{1,0:T(8,128)(2,1)} fusion(bf16[2048,512]{1,0:T(8,128)(2,1)S(1)} %bitcast.20, s32[2048]{0:T(1024)S(1)} %pad_clamp_fusion), kind=kCustom, calls=%fused_computation.1 | custom fusion | bytes 3677184 | tf_op jit(solution)/shard_map/gather | solution.py:48
  280.8 3.6 convert_reduce_fusion
  284.4 4.2 convolution_bitcast_fusion
  288.6 239.4 %all-reduce.4 = (bf16[1024,512]{0,1:T(8,128)(2,1)}, f32[512]{0:T(512)}) all-reduce(f32[1024,512]{0,1:T(8,128)S(1)} %convolution_bitcast_fusion, f32[512]{0:T(512)S(1)} %get-tuple-element.8), channel_id=1, replica_groups=mesh['dp'=32,'mp'=16] {'dp'}, use_global_device_ids=true, to_apply=%region_3.0 | all-reduce | flops 524800 | bytes 3149824 | tf_op jit(solution)/shard_map/psum | solution.py:54
  527.9 2.3 copy.10
  (6 shorter events, 0.0 us)
Async XLA Ops:
  0.6 125.2 %copy-start = (bf16[1024,512]{1,0:T(8,128)(2,1)S(1)}, bf16[1024,512]{1,0:T(8,128)(2,1)}, u32[]{:S(2)}) copy-start(bf16[1024,512]{1,0:T(8,128)(2,1)} %param.8) | copy-start | bytes 3145732
  4.0 17.8 %copy-start.4 = (s32[112]{0:T(128)S(1)}, s32[112]{0:T(128)}, u32[]{:S(2)}) copy-start(s32[112]{0:T(128)} %param.7) | copy-start | bytes 1348
  4.0 121.9 %copy-start.3 = (f32[512]{0:T(512)S(1)}, f32[512]{0:T(512)}, u32[]{:S(2)}) copy-start(f32[512]{0:T(512)} %param.9) | copy-start | bytes 6148
  4.0 121.9 %all-to-all-start = ((bf16[16,112,1024]{2,1,0:T(8,128)(2,1)}), bf16[16,112,1024]{2,1,0:T(8,128)(2,1)}, u32[]{:S(2)}, u32[]{:S(2)}) async-start(bf16[16,112,1024]{2,1,0:T(8,128)(2,1)} %stack.2), calls=%async_computation | async-start | bytes 7340032 | tf_op jit(solution)/shard_map/all_to_all | solution.py:10
  141.0 63.4 %copy-start.1 = (bf16[128,8192]{1,0:T(8,128)(2,1)S(1)}, bf16[128,8192]{1,0:T(8,128)(2,1)}, u32[]{:S(2)}) copy-start(bf16[128,8192]{1,0:T(8,128)(2,1)} %param.11) | copy-start | bytes 6291460
  141.0 63.4 %copy-start.2 = (f32[8192]{0:T(1024)S(1)}, f32[8192]{0:T(1024)}, u32[]{:S(2)}) copy-start(f32[8192]{0:T(1024)} %param.10) | copy-start | bytes 98308
  208.6 66.0 %all-to-all-start.2 = ((bf16[128,16,512]{2,0,1:T(8,128)(2,1)}), bf16[128,16,512]{2,0,1:T(8,128)(2,1)S(1)}, u32[]{:S(2)}, u32[]{:S(2)}) async-start(bf16[128,16,512]{2,0,1:T(8,128)(2,1)} %bitcast.24), calls=%async_computation.2 | async-start | bytes 4194304 | tf_op jit(solution)/shard_map/all_to_all | solution.py:47
